TPU v7x, 512 devices: a whole 4x4x16 slice. The times are simulated.
512 devices in a mesh: bulk: 32 (over z, core), blk: 16 (over y, x).
Axes of the slice: x: 4, y: 4, z: 16, core: 2. Of those that a mesh axis runs over, the one named last changes fastest.
Arguments:
- factor: float32 [131072, 4096], P(('bulk', 'blk')), parts along dimension 0, as said below
- initial: float32 [131072, 128], P(('bulk', 'blk')), parts along dimension 0, may hold values from -6 to 6
- bounds: float32 [64], P('bulk'), parts along dimension 0, may hold values from 0 to 15.5, as said below
Outputs:
- basis_rows: float32 [131072, 128], P(('bulk', 'blk')), parts along dimension 0
- projected: float32 [4096, 128], P('bulk'), parts along dimension 0
- residual: float32 [131072, 128], P(('bulk', 'blk')), parts along dimension 0
There are 32 independent parts, one for each index of `bulk`. A program takes and returns all parts, laid end to end along the dimension named above; each array names one. Nothing has to cross between parts.
Inputs may be any that keep to these rules, and one draw needn't show every extreme that they name: factor is symmetric. `bounds`: the upper end exceeds the lower end by 14 or more.
All inputs are finite; a program needn't handle non-finite values.
Results may differ from a plain program's by a relative error of at most 0.0003.
Values sent between devices are 32-bit elements; how exact they have to be, the bound alone decides.
A program may use at most 64 MiB of HBM per device.

v0:
```python
import jax
import jax.numpy as jnp
from jax import lax
from jax.sharding import PartitionSpec as P

DEGREE = 8


def local_dot(left_side, right_side):
    return jnp.dot(
        left_side, right_side, precision=lax.Precision.HIGHEST, preferred_element_type=jnp.float32
    )


def lower_solve(cholesky_low, right_side):
    return lax.linalg.triangular_solve(cholesky_low, right_side, left_side=True, lower=True)


def apply_factor(factor_rows, vectors):
    return local_dot(factor_rows, lax.all_gather(vectors, "blk", axis=0, tiled=True))


def local(factor, initial, bounds):
    centre = (bounds[0] + bounds[1]) / 2.0
    radius = (bounds[1] - bounds[0]) / 2.0
    previous = initial
    current = (apply_factor(factor, initial) - centre * initial) / radius
    for order_step in range(DEGREE - 1):
        scaled = (apply_factor(factor, current) - centre * current) / radius
        following = 2.0 * scaled - previous
        previous = current
        current = following
    gram_matrix = lax.psum(
        lax.dot_general(
            current,
            current,
            (((0,), (0,)), ((), ())),
            precision=lax.Precision.HIGHEST,
            preferred_element_type=jnp.float32,
        ),
        "blk",
    )
    cholesky_low = jnp.linalg.cholesky(gram_matrix)
    basis_rows = lower_solve(cholesky_low, current.T).T
    mapped = apply_factor(factor, basis_rows)
    projected = lax.psum(
        lax.dot_general(
            basis_rows,
            mapped,
            (((0,), (0,)), ((), ())),
            precision=lax.Precision.HIGHEST,
            preferred_element_type=jnp.float32,
        ),
        "blk",
    )
    residual = mapped - local_dot(basis_rows, projected)
    return (basis_rows, projected, residual)


def solution(mesh):
    in_specs = (P(("bulk", "blk"), None), P(("bulk", "blk"), None), P("bulk"))
    out_specs = (P(("bulk", "blk"), None), P("bulk", None), P(("bulk", "blk"), None))
    return jax.shard_map(local, mesh=mesh, in_specs=in_specs, out_specs=out_specs, check_vma=False)
```

profile of v0, /device:TPU:2, one launch (start us, length us, event | category | flops | bytes accessed | tf_op | source)
XLA Modules:
  0.0 880.1 jit_solution(10453286735526572936)
XLA Ops:
  7.2 0.0 all-gather.10.cloned.1.call-start
  7.2 0.7 all-gather.10.cloned.1.call-update
  7.9 0.0 all-gather.12.cloned.1.call-start
  7.9 1.3 fusion.33
  11.9 63.6 %all-gather.10.cloned.1.call-done = f32[4096,128]{1,0:T(8,128)} async-done(((f32[256,128]{1,0:T(8,128)}), f32[4096,128]{1,0:T(8,128)}) %all-gather.10.cloned.1.call-update) | async-done | bytes 2097168 | tf_op jit(solution)/shard_map/all_gather | solution.py:20
  75.4 7.0 fusion.28
  82.4 0.0 all-gather.12.cloned.1.call-update
  82.4 0.0 all-gather.14.cloned.1.call-start
  82.5 59.8 %all-gather.12.cloned.1.call-done = f32[4096,128]{1,0:T(8,128)} async-done(((f32[256,128]{1,0:T(8,128)}), f32[4096,128]{1,0:T(8,128)}) %all-gather.12.cloned.1.call-update) | async-done | bytes 2097168 | tf_op jit(solution)/shard_map/all_gather | solution.py:20
  142.3 7.0 fusion.27
  149.2 0.0 all-gather.14.cloned.1.call-update
  149.3 0.0 all-gather.16.cloned.1.call-start
  149.3 59.8 %all-gather.14.cloned.1.call-done = f32[4096,128]{1,0:T(8,128)} async-done(((f32[256,128]{1,0:T(8,128)}), f32[4096,128]{1,0:T(8,128)}) %all-gather.14.cloned.1.call-update) | async-done | bytes 2097168 | tf_op jit(solution)/shard_map/all_gather | solution.py:20
  209.1 7.0 fusion.23
  216.1 0.2 all-gather.18.cloned.1.call-start
  216.3 59.6 %all-gather.16.cloned.1.call-done = f32[4096,128]{1,0:T(8,128)} async-done(((f32[256,128]{1,0:T(8,128)}), f32[4096,128]{1,0:T(8,128)}) %all-gather.16.cloned.1.call-update) | async-done | bytes 2097168 | tf_op jit(solution)/shard_map/all_gather | solution.py:20
  276.0 7.0 fusion.19
  283.0 0.0 all-gather.20.cloned.1.call-start
  283.0 59.8 %all-gather.18.cloned.1.call-done = f32[4096,128]{1,0:T(8,128)} async-done(((f32[256,128]{1,0:T(8,128)}), f32[4096,128]{1,0:T(8,128)}) %all-gather.18.cloned.1.call-update) | async-done | bytes 2097168 | tf_op jit(solution)/shard_map/all_gather | solution.py:20
  342.8 7.0 fusion.15
  349.8 0.0 all-gather.22.cloned.1.call-start
  349.9 59.8 %all-gather.20.cloned.1.call-done = f32[4096,128]{1,0:T(8,128)} async-done(((f32[256,128]{1,0:T(8,128)}), f32[4096,128]{1,0:T(8,128)}) %all-gather.20.cloned.1.call-update) | async-done | bytes 2097168 | tf_op jit(solution)/shard_map/all_gather | solution.py:20
  409.7 7.0 fusion.11
  416.7 0.3 all-gather.24.cloned.1.call-start
  416.9 59.6 %all-gather.22.cloned.1.call-done = f32[4096,128]{1,0:T(8,128)} async-done(((f32[256,128]{1,0:T(8,128)}), f32[4096,128]{1,0:T(8,128)}) %all-gather.22.cloned.1.call-update) | async-done | bytes 2097168 | tf_op jit(solution)/shard_map/all_gather | solution.py:20
  476.5 7.0 fusion.7
  483.5 0.0 all-reduce.3.cloned.1.call-start
  483.6 59.8 %all-gather.24.cloned.1.call-done = f32[4096,128]{1,0:T(8,128)} async-done(((f32[256,128]{1,0:T(8,128)}), f32[4096,128]{1,0:T(8,128)}) %all-gather.24.cloned.1.call-update) | async-done | bytes 2097168 | tf_op jit(solution)/shard_map/all_gather | solution.py:20
  543.4 6.3 fusion.3
  549.7 1.0 fusion.34
  550.7 0.3 all-gather.26.cloned.1.call-start
  551.0 111.0 %all-reduce.3.cloned.1.call-done = f32[128,128]{0,1:T(8,128)} async-done(((f32[128,128]{0,1:T(8,128)}), f32[128,128]{0,1:T(8,128)}) %all-reduce.3.cloned.1.call-update) | async-done | bytes 65552 | tf_op jit(solution)/shard_map/psum | solution.py:33
  662.0 0.9 copy.14
  662.9 0.9 fusion.32
  663.8 11.7 %cholesky.16 = f32[128,128]{1,0:T(8,128)S(1)} custom-call(f32[128,128]{1,0:T(8,128)S(1)} %fusion.32), custom_call_target="Cholesky" | custom-call | tf_op jit(solution)/shard_map/jit(cholesky)/cholesky | solution.py:43
  675.5 0.6 compare_reduce_fusion
  676.2 0.7 fusion.29
  676.8 9.8 %custom-call.6 = f32[1,128,128]{1,2,0:T(8,128)S(1)} custom-call(f32[1,128,128]{2,1,0:T(8,128)S(1)} %fusion.29), custom_call_target="InvertDiagBlocksLowerTriangular" | custom-call | tf_op jit(solution)/shard_map/triangular_solve | solution.py:16
  686.7 1.0 fusion.30
  687.7 0.0 all-reduce.5.cloned.1.call-start
  687.7 62.6 %all-gather.26.cloned.1.call-done = f32[4096,128]{0,1:T(8,128)} async-done(((f32[256,128]{0,1:T(8,128)}), f32[4096,128]{0,1:T(8,128)}) %all-gather.26.cloned.1.call-update) | async-done | bytes 2097168 | tf_op jit(solution)/shard_map/all_gather | solution.py:20
  750.3 7.1 fusion.35
  757.4 0.9 fusion.36
  758.3 0.8 copy.16
  759.1 110.6 %all-reduce.5.cloned.1.call-done = f32[128,128]{1,0:T(8,128)} async-done(((f32[128,128]{1,0:T(8,128)}), f32[128,128]{1,0:T(8,128)}) %all-reduce.5.cloned.1.call-update) | async-done | bytes 65552 | tf_op jit(solution)/shard_map/psum | solution.py:46
  869.7 1.2 convolution_subtract_fusion.1
  870.9 0.8 copy.17
  871.6 1.5 copy.29
  (25 shorter events, 0.2 us)
Async XLA Ops:
  7.2 68.3 %all-gather.10.cloned.1.call-start = ((), (), s32[]{:S(2)}) async-start(), calls=%async_computation | async-start | bytes 2228224 | tf_op jit(solution)/shard_map/all_gather | solution.py:20
  7.9 134.4 %all-gather.12.cloned.1.call-start = ((), (), s32[]{:S(2)}) async-start(), calls=%async_computation.1 | async-start | bytes 2228224 | tf_op jit(solution)/shard_map/all_gather | solution.py:20
  75.4 66.9 %copy-start.7 = (f32[256,128]{1,0:T(8,128)S(1)}, f32[256,128]{1,0:T(8,128)}, u32[]{:S(2)}) copy-start(f32[256,128]{1,0:T(8,128)} %param.4) | copy-start | bytes 393220
  82.4 126.7 %copy-start.6 = (f32[256,128]{1,0:T(8,128)S(1)}, f32[256,128]{1,0:T(8,128)}, u32[]{:S(2)}) copy-start(f32[256,128]{1,0:T(8,128)} %fusion.28) | copy-start | bytes 393220
  82.4 126.7 %all-gather.14.cloned.1.call-start = ((), (), s32[]{:S(2)}) async-start(), calls=%async_computation.2 | async-start | bytes 2228224 | tf_op jit(solution)/shard_map/all_gather | solution.py:20
  149.3 126.7 %copy-start.5 = (f32[256,128]{1,0:T(8,128)S(1)}, f32[256,128]{1,0:T(8,128)}, u32[]{:S(2)}) copy-start(f32[256,128]{1,0:T(8,128)} %fusion.27) | copy-start | bytes 393220
  149.3 126.7 %all-gather.16.cloned.1.call-start = ((), (), s32[]{:S(2)}) async-start(), calls=%async_computation.3 | async-start | bytes 2228224 | tf_op jit(solution)/shard_map/all_gather | solution.py:20
  216.1 126.7 %copy-start.2 = (f32[256,128]{1,0:T(8,128)S(1)}, f32[256,128]{1,0:T(8,128)}, u32[]{:S(2)}) copy-start(f32[256,128]{1,0:T(8,128)} %fusion.23) | copy-start | bytes 393220
  216.1 126.7 %all-gather.18.cloned.1.call-start = ((), (), s32[]{:S(2)}) async-start(), calls=%async_computation.4 | async-start | bytes 2228224 | tf_op jit(solution)/shard_map/all_gather | solution.py:20
  283.0 126.7 %copy-start.3 = (f32[256,128]{1,0:T(8,128)S(1)}, f32[256,128]{1,0:T(8,128)}, u32[]{:S(2)}) copy-start(f32[256,128]{1,0:T(8,128)} %fusion.19) | copy-start | bytes 393220
  283.0 126.7 %all-gather.20.cloned.1.call-start = ((), (), s32[]{:S(2)}) async-start(), calls=%async_computation.5 | async-start | bytes 2228224 | tf_op jit(solution)/shard_map/all_gather | solution.py:20
  349.8 126.7 %copy-start.4 = (f32[256,128]{1,0:T(8,128)S(1)}, f32[256,128]{1,0:T(8,128)}, u32[]{:S(2)}) copy-start(f32[256,128]{1,0:T(8,128)} %fusion.15) | copy-start | bytes 393220
  349.8 126.7 %all-gather.22.cloned.1.call-start = ((), (), s32[]{:S(2)}) async-start(), calls=%async_computation.6 | async-start | bytes 2228224 | tf_op jit(solution)/shard_map/all_gather | solution.py:20
  416.7 126.7 %copy-start.1 = (f32[256,128]{1,0:T(8,128)S(1)}, f32[256,128]{1,0:T(8,128)}, u32[]{:S(2)}) copy-start(f32[256,128]{1,0:T(8,128)} %fusion.11) | copy-start | bytes 393220
  416.7 126.7 %all-gather.24.cloned.1.call-start = ((), (), s32[]{:S(2)}) async-start(), calls=%async_computation.7 | async-start | bytes 2228224 | tf_op jit(solution)/shard_map/all_gather | solution.py:20
  483.5 178.5 %all-reduce.3.cloned.1.call-start = ((), (), s32[]{:S(2)}) async-start(), calls=%async_computation.8 | async-start | bytes 131072 | tf_op jit(solution)/shard_map/psum | solution.py:33
  550.7 199.6 %all-gather.26.cloned.1.call-start = ((), (), s32[]{:S(2)}) async-start(), calls=%async_computation.9 | async-start | bytes 2228224 | tf_op jit(solution)/shard_map/all_gather | solution.py:20
  687.7 69.7 %copy-start = (f32[128,256]{1,0:T(8,128)S(1)}, f32[128,256]{1,0:T(8,128)}, u32[]{:S(2)}) copy-start(f32[128,256]{1,0:T(8,128)} %fusion.30) | copy-start | bytes 393220
  687.7 182.0 %all-reduce.5.cloned.1.call-start = ((), (), s32[]{:S(2)}) async-start(), calls=%async_computation.10 | async-start | bytes 131072 | tf_op jit(solution)/shard_map/psum | solution.py:46
Sparse Core Ops, SparseCore 0:
  11.0 64.3 all-gather.9
  82.5 59.6 all-gather.11
  149.4 59.6 all-gather.13
  216.2 59.6 all-gather.15
  283.1 59.6 all-gather.17
  349.9 59.6 all-gather.19
  416.8 59.6 all-gather.21
  483.6 59.6 all-gather.23
  550.8 111.1 all-reduce.2
  687.8 62.4 all-gather.25
  758.5 111.1 all-reduce.4
where the time goes:
time: 888 us; the launch traced here: 880 us
  waiting for transfers between devices  767 us (86%)
  matrix products  66.2 us (7%)
  other arithmetic  23.7 us (3%)
  between operations  17 us (2%)
    all_gather x9, waiting for transfers between devices, apply_factor(): lax.all_gather(vectors, 'blk', axis=0, tiled=True)  544 us
    psum x1, waiting for transfers between devices, local(): lax.psum(lax.dot_general(current, current, (((0,), (0,)), ((), ())), prec...  111 us
    psum x1, waiting for transfers between devices, local(): lax.psum(lax.dot_general(basis_rows, mapped, (((0,), (0,)), ((), ())), pr...  111 us
    dot_general x10, matrix products, local_dot(): jnp.dot(left_side, right_side, precision=lax.Precision.HIGHEST, preferred...  63.3 us
  transfers between devices with their start and end apart: 11, of which 11 were waited for; matrix products, arithmetic and copies ran while one was open for 0% of the time, Pallas kernels for 0%

commit v1 on v0

v1 whole, which is shorter than its diff:
```python
import functools

import jax
import jax.numpy as jnp
from jax import lax
from jax.experimental import pallas as pl
from jax.experimental.pallas import tpu as pltpu
from jax.sharding import PartitionSpec as P

DEGREE = 8
SIDE = 4
CHAINS = 4
PANEL = 32
X, Y = 0, 1
FIRST = (X, Y, X, Y)
MESH = pl.DeviceIdType.MESH
F32, BF16 = jnp.float32, jnp.bfloat16
HIGHEST = lax.Precision.HIGHEST
NN = (((1,), (0,)), ((), ()))
NT = (((1,), (1,)), ((), ()))
TN = (((0,), (0,)), ((), ()))

OVER_X = ((1, 1), (3, 3), (2, 1), (2, 3))
OVER_Y = ((1, 3), (3, 1), (1, 2), (3, 2))


def exact_dot(left, right, dims):
    return lax.dot_general(left, right, dims, precision=HIGHEST, preferred_element_type=F32)


def xor(value, k):
    if k == 0:
        return value
    if k == 1:
        return value + 1 - 2 * (value % 2)
    if k == 2:
        return (value + 2) % 4
    return 3 - value


def split(value):
    high = value.astype(BF16)
    low = (value - high.astype(F32)).astype(BF16)
    return high, low


def kernel(
    factor, initial, bounds,
    basis_out, projected_out, residual_out,
    own_rows, arrived, arrived_half, w_high, w_low, vectors, stacked, partial_own, partial_out, partial_in, gathered,
    small_out, small_in, work,
    own_sem, block_send, block_recv, rs_send, rs_recv, ag_send, ag_recv, small_send, small_recv,
):
    me = lax.axis_index("blk")
    my_y, my_x = me // SIDE, me % SIDE
    nb = own_rows.shape[0]
    kc = partial_own.shape[1]
    k_all = CHAINS * kc

    def peer(axis, k):
        if axis == X:
            return {"blk": my_y * SIDE + xor(my_x, k)}
        return {"blk": xor(my_y, k) * SIDE + my_x}

    def column(ky, kx):
        return pl.multiple_of((xor(my_y, ky) * SIDE + xor(my_x, kx)) * nb, nb)

    def remote(src, dst, send, recv, axis, k):
        return pltpu.make_async_remote_copy(
            src_ref=src, dst_ref=dst, send_sem=send, recv_sem=recv, device_id=peer(axis, k), device_id_type=MESH
        )

    own_copy = pltpu.make_async_copy(factor, own_rows, own_sem)
    own_copy.start()
    vectors[0] = jnp.zeros((k_all, nb), F32)
    vectors[1] = initial[...].T

    barrier = pltpu.get_barrier_semaphore()
    for axis in (X, Y):
        for k in (1, 2, 3):
            pl.semaphore_signal(barrier, inc=1, device_id=peer(axis, k), device_id_type=MESH)
    pl.semaphore_wait(barrier, 6)

    def rows_of(chain):
        return pl.ds(chain * kc, kc)

    def rs_copy(chain, axis, k):
        return remote(
            partial_out.at[chain, axis, k], partial_in.at[chain, axis, k],
            rs_send.at[chain, axis, k], rs_recv.at[chain, axis, k], axis, k,
        )

    def ag_copy(chain, axis, k, order):
        return remote(
            vectors.at[order + 1, rows_of(chain)], gathered.at[chain, axis, k],
            ag_send.at[chain, axis, k], ag_recv.at[chain, axis, k], axis, k,
        )

    def block_copy(ky, kx, axis):
        return remote(
            factor.at[:, pl.ds(column(ky, kx), nb)], arrived.at[ky, kx],
            block_send.at[ky, kx], block_recv.at[ky, kx], axis, kx if axis == X else ky,
        )

    half = nb // 2
    top_copy = remote(
        factor.at[pl.ds(0, half), pl.ds(column(2, 2), nb)], arrived.at[2, 2, pl.ds(0, half)],
        block_send.at[2, 2], block_recv.at[2, 2], X, 2,
    )
    side_copy = remote(
        factor.at[:, pl.ds(pl.multiple_of(column(2, 2) + half, half), half)], arrived_half,
        block_send.at[0, 0], block_recv.at[0, 0], Y, 2,
    )

    for chain in range(CHAINS):
        for k in (2, 1, 3):
            ag_copy(chain, 1 - FIRST[chain], k, 0).start()
    block_copies = []
    for over_x, over_y in zip(OVER_X, OVER_Y):
        block_copies += [(over_x, X), (over_y, Y)]
    for (ky, kx), axis in block_copies:
        block_copy(ky, kx, axis).start()
    top_copy.start()
    side_copy.start()

    def put(axis, k_out, k_in, rows, columns, value):
        high, low = split(value)
        w_high[axis, k_out, pl.ds(k_in * nb + rows[0], rows[1]), pl.ds(columns[0], columns[1])] = high
        w_low[axis, k_out, pl.ds(k_in * nb + rows[0], rows[1]), pl.ds(columns[0], columns[1])] = low

    whole = (0, nb)

    def place(ky, kx, value, axis):
        if axis == X:
            put(Y, ky, kx, whole, whole, value)
            put(X, kx, ky, whole, whole, value.T)
        else:
            put(X, kx, ky, whole, whole, value)
            put(Y, ky, kx, whole, whole, value.T)

    own_copy.wait()
    for k in range(SIDE):
        place(k, 0, own_rows[:, pl.ds(column(k, 0), nb)], X)
        if k:
            place(0, k, own_rows[:, pl.ds(column(0, k), nb)], Y)
    for (ky, kx), axis in block_copies:
        block_copy(ky, kx, axis).wait_recv()
        place(ky, kx, arrived[ky, kx], axis)
    top_copy.wait_recv()
    top = arrived[2, 2, pl.ds(0, half)]
    put(Y, 2, 2, (0, half), whole, top)
    put(X, 2, 2, whole, (0, half), top.T)
    side_copy.wait_recv()
    side = arrived_half[...]
    put(X, 2, 2, whole, (half, half), side)
    put(Y, 2, 2, (half, half), whole, side.T)

    low_end, high_end = bounds[0], bounds[1]
    centre = (low_end + high_end) / 2.0
    radius = (high_end - low_end) / 2.0

    def stack(chain, k, value):
        high, low = split(value)
        stacked[chain, pl.ds(0, kc), pl.ds(k * nb, nb)] = high
        stacked[chain, pl.ds(kc, kc), pl.ds(k * nb, nb)] = low

    def multiply(chain, axis, order):
        along = 1 - axis
        stack(chain, 0, vectors[order + 1, rows_of(chain)])
        for k in (1, 3, 2):
            ag_copy(chain, along, k, order).wait_recv()
            stack(chain, k, gathered[chain, along, k])
        for k in (2, 1, 3, 0):
            both = lax.dot_general(stacked[chain], w_high[axis, k], NN, preferred_element_type=F32)
            rest = lax.dot_general(stacked[chain, pl.ds(0, kc)], w_low[axis, k], NN, preferred_element_type=F32)
            part = both[:kc] + (both[kc:] + rest)
            if k:
                partial_out[chain, axis, k] = part
                rs_copy(chain, axis, k).start()
            else:
                partial_own[chain] = part
        for k in (1, 2, 3):
            ag_copy(chain, along, k, order).wait_send()

    def total(chain, axis):
        for k in (1, 3, 2):
            rs_copy(chain, axis, k).wait_recv()
        return (partial_own[chain] + partial_in[chain, axis, 1]) + (partial_in[chain, axis, 2] + partial_in[chain, axis, 3])

    def advance(chain, axis, order, twice):
        product = total(chain, axis)
        current = vectors[order + 1, rows_of(chain)]
        scaled = (product - centre * current) / radius
        vectors[order + 2, rows_of(chain)] = twice * scaled - vectors[order, rows_of(chain)]
        for k in (2, 1, 3):
            ag_copy(chain, axis, k, order + 1).start()
        for k in (1, 2, 3):
            rs_copy(chain, axis, k).wait_send()

    def pair(step, carry):
        for later in (0, 1):
            order = 2 * step + later
            twice = jnp.where(order == 0, 1.0, 2.0)
            for chain in range(CHAINS):
                multiply(chain, (FIRST[chain] + later) % 2, order)
            for chain in range(CHAINS):
                advance(chain, (FIRST[chain] + later) % 2, order, twice)
        return carry

    lax.fori_loop(0, DEGREE // 2, pair, 0)

    hk = k_all // 2

    def small_copy(which, stage, part, k):
        axis = (part + stage) % 2
        return remote(
            small_out.at[which, stage, pl.ds(part * hk, hk)], small_in.at[which, stage, k, pl.ds(part * hk, hk)],
            small_send.at[which, stage, part, k], small_recv.at[which, stage, part, k], axis, k,
        )

    def small_start(which, stage):
        for k in (2, 1, 3):
            for part in (0, 1):
                small_copy(which, stage, part, k).start()

    def small_sum(which, stage):
        for k in (1, 3, 2):
            for part in (0, 1):
                small_copy(which, stage, part, k).wait_recv()
        return (small_out[which, stage] + small_in[which, stage, 1]) + (small_in[which, stage, 2] + small_in[which, stage, 3])

    filtered = vectors[DEGREE + 1]
    small_out[0, 0] = exact_dot(filtered, filtered, NT)
    small_start(0, 0)
    for chain in range(CHAINS):
        multiply(chain, FIRST[chain], DEGREE)
    small_out[0, 1] = small_sum(0, 0)
    small_start(0, 1)
    for chain in range(CHAINS):
        vectors[0, rows_of(chain)] = total(chain, FIRST[chain])
    gram = small_sum(0, 1)

    row_at = lax.broadcasted_iota(jnp.int32, (k_all, k_all), 0)
    column_at = lax.broadcasted_iota(jnp.int32, (k_all, k_all), 1)
    diagonal = jnp.where(row_at == column_at, gram, 0.0)
    scale_rows = lax.rsqrt(jnp.sum(diagonal, axis=1, keepdims=True))
    scale_columns = lax.rsqrt(jnp.sum(diagonal, axis=0, keepdims=True))
    filtered = filtered * scale_rows
    image = vectors[0] * scale_rows
    small_out[1, 0] = exact_dot(filtered, image, NT)
    small_start(1, 0)

    work[:, pl.ds(0, k_all)] = gram * scale_rows * scale_columns
    work[:, pl.ds(k_all, k_all)] = jnp.where(row_at == column_at, 1.0, 0.0)
    panel_row = lax.broadcasted_iota(jnp.int32, (PANEL, 1), 0)

    def eliminate(panel):
        rows = pl.ds(panel * PANEL, PANEL)
        block = work[rows, :]
        for j in range(PANEL):
            at = panel * PANEL + j
            inverse = lax.rsqrt(block[j : j + 1, at : at + 1])
            pivot_row = block[j : j + 1, :] * inverse
            multiplier = jnp.where(panel_row > j, block[:, at : at + 1] * inverse, 0.0)
            block = jnp.where(panel_row == j, pivot_row, block - multiplier * pivot_row)
        work[rows, :] = block
        done = (panel + 1) * PANEL
        if done < k_all:
            below = pl.ds(done, k_all - done)
            work[below, :] = work[below, :] - exact_dot(block[:, done:k_all], block, TN)

    panels = k_all // PANEL
    for panel in range(panels // 2):
        eliminate(panel)
    small_out[1, 1] = small_sum(1, 0)
    small_start(1, 1)
    for panel in range(panels // 2, panels):
        eliminate(panel)
    inverse_low = work[:, pl.ds(k_all, k_all)]
    basis = exact_dot(inverse_low, filtered, NN)
    mapped = exact_dot(inverse_low, image, NN)
    basis_out[...] = basis.T
    inner = small_sum(1, 1)
    projected = exact_dot(exact_dot(inverse_low, inner, NN), inverse_low, NT)
    projected_out[...] = projected
    residual_out[...] = (mapped - exact_dot(projected, basis, TN)).T

    for (ky, kx), axis in block_copies:
        block_copy(ky, kx, axis).wait_send()
    top_copy.wait_send()
    side_copy.wait_send()
    for chain in range(CHAINS):
        for k in (1, 2, 3):
            rs_copy(chain, FIRST[chain], k).wait_send()
    for which in (0, 1):
        for stage in (0, 1):
            for part in (0, 1):
                for k in (1, 2, 3):
                    small_copy(which, stage, part, k).wait_send()


def local(factor, initial, bounds):
    nb, k_all = initial.shape
    kc = k_all // CHAINS
    vmem = pl.BlockSpec(memory_space=pltpu.VMEM)
    dma = pltpu.SemaphoreType.DMA
    return pl.pallas_call(
        kernel,
        out_shape=(
            jax.ShapeDtypeStruct((nb, k_all), F32),
            jax.ShapeDtypeStruct((k_all, k_all), F32),
            jax.ShapeDtypeStruct((nb, k_all), F32),
        ),
        in_specs=[pl.BlockSpec(memory_space=pl.ANY), vmem, pl.BlockSpec(memory_space=pltpu.SMEM)],
        out_specs=(vmem, vmem, vmem),
        scratch_shapes=[
            pltpu.VMEM((nb, SIDE * SIDE * nb), F32),
            pltpu.VMEM((SIDE, SIDE, nb, nb), F32),
            pltpu.VMEM((nb, nb // 2), F32),
            pltpu.VMEM((2, SIDE, SIDE * nb, nb), BF16),
            pltpu.VMEM((2, SIDE, SIDE * nb, nb), BF16),
            pltpu.VMEM((DEGREE + 2, k_all, nb), F32),
            pltpu.VMEM((CHAINS, 2 * kc, SIDE * nb), BF16),
            pltpu.VMEM((CHAINS, kc, nb), F32),
            pltpu.VMEM((CHAINS, 2, SIDE, kc, nb), F32),
            pltpu.VMEM((CHAINS, 2, SIDE, kc, nb), F32),
            pltpu.VMEM((CHAINS, 2, SIDE, kc, nb), F32),
            pltpu.VMEM((2, 2, k_all, k_all), F32),
            pltpu.VMEM((2, 2, SIDE, k_all, k_all), F32),
            pltpu.VMEM((k_all, 2 * k_all), F32),
            dma,
            dma((SIDE, SIDE)),
            dma((SIDE, SIDE)),
            dma((CHAINS, 2, SIDE)),
            dma((CHAINS, 2, SIDE)),
            dma((CHAINS, 2, SIDE)),
            dma((CHAINS, 2, SIDE)),
            dma((2, 2, 2, SIDE)),
            dma((2, 2, 2, SIDE)),
        ],
        compiler_params=pltpu.CompilerParams(collective_id=0, has_side_effects=True, vmem_limit_bytes=48 << 20),
    )(factor, initial, bounds)


def solution(mesh):
    in_specs = (P(("bulk", "blk"), None), P(("bulk", "blk"), None), P("bulk"))
    out_specs = (P(("bulk", "blk"), None), P("bulk", None), P(("bulk", "blk"), None))
    return jax.shard_map(local, mesh=mesh, in_specs=in_specs, out_specs=out_specs, check_vma=False)
```

time: 888 us -> 149 us (0.17)
  the two profiles are of different devices: /device:TPU:2 before, /device:TPU:448 now
where the time goes in v1:
time: 149 us
  Pallas kernels  142 us (95%)
  local copies, waits for them, and re-layouts  5.68 us (4%)
    pallas_call x1, Pallas kernels, local(): pl.pallas_call(kernel, out_shape=(jax.ShapeDtypeStruct((nb, k_all), F32),...  142 us
    unnamed x9, local copies, waits for them, and re-layouts  5.68 us

profile of v1, /device:TPU:448, one launch (start us, length us, event | category | flops | bytes accessed | tf_op | source)
XLA Modules:
  0.0 148.6 jit_solution(16213747723163935541)
XLA Ops:
  0.6 0.0 copy-start
  0.6 2.2 %copy-done = f32[256,4096]{1,0:T(8,128)S(1)} copy-done((f32[256,4096]{1,0:T(8,128)S(1)}, f32[256,4096]{1,0:T(8,128)}, u32[]{:S(2)}) %copy-start) | copy-done | bytes 4194328
  2.8 0.0 copy-start.1
  2.8 0.9 copy-done.1
  3.7 0.0 copy-start.2
  3.7 0.7 copy-done.2
  4.4 142.3 %shard_map.58 = (f32[256,128]{1,0:T(8,128)S(1)}, f32[128,128]{1,0:T(8,128)S(1)}, f32[256,128]{1,0:T(8,128)S(1)}) custom-call(f32[256,4096]{1,0:T(8,128)S(1)} %copy-done, f32[256,128]{1,0:T(8,128)S(1)} %copy-done.1, f32[2]{0:T(128)S(1)} %copy-done.2), custom_call_target="tpu_custom_call" | custom-call | tf_op jit(solution)/shard_map/pallas_call | solution.py:307
  146.7 0.7 copy.9
  147.4 0.6 copy.10
  148.0 0.7 copy.11
Async XLA Ops:
  0.6 2.2 %copy-start = (f32[256,4096]{1,0:T(8,128)S(1)}, f32[256,4096]{1,0:T(8,128)}, u32[]{:S(2)}) copy-start(f32[256,4096]{1,0:T(8,128)} %factor.1) | copy-start | bytes 12582916
  2.8 0.9 copy-start.1
  3.7 0.7 copy-start.2

commit v2 on v1

v2 whole, which is shorter than its diff:
```python
import functools

import jax
import jax.numpy as jnp
from jax import lax
from jax.experimental import pallas as pl
from jax.experimental.pallas import tpu as pltpu
from jax.sharding import PartitionSpec as P

DEGREE = 8
SIDE = 4
CHAINS = 4
PANEL = 32
GROUP = 16
DOWN = 2.0**-12
X, Y = 0, 1
FIRST = (X, Y, X, Y)
MESH = pl.DeviceIdType.MESH
F32, BF16 = jnp.float32, jnp.bfloat16
HIGHEST = lax.Precision.HIGHEST
NN = (((1,), (0,)), ((), ()))
NT = (((1,), (1,)), ((), ()))
TN = (((0,), (0,)), ((), ()))

OVER_X = ((1, 1), (3, 3), (2, 1), (2, 3))
OVER_Y = ((1, 3), (3, 1), (1, 2), (3, 2))
LOCAL = ((0, 0), (1, 0), (2, 0), (3, 0), (0, 1), (0, 2), (0, 3))


def exact_dot(left, right, dims):
    return lax.dot_general(left, right, dims, precision=HIGHEST, preferred_element_type=F32)


def xor(value, k):
    if k == 0:
        return value
    if k == 1:
        return value + 1 - 2 * (value % 2)
    if k == 2:
        return (value + 2) % 4
    return 3 - value


def split(value):
    high = value.astype(BF16)
    low = (value - high.astype(F32)).astype(BF16)
    return high, low


def kernel(
    factor, initial, bounds,
    basis_out, projected_out, residual_out,
    own_blocks, arrived, arrived_half, start, w_high, w_low, vectors, stacked, partial, sums, from_first, from_second,
    last_in, image_own, small_out, small_in, work, staged,
    own_sem, block_send, block_recv, x_send, x_recv, last_send, last_recv, small_send, small_recv,
):
    me = lax.axis_index("blk")
    my_y, my_x = me // SIDE, me % SIDE
    nb, k_all = start.shape[1], start.shape[0]
    kc = k_all // CHAINS
    hc = kc // 2
    half = nb // 2

    def peer(axis, k):
        if axis == X:
            return {"blk": my_y * SIDE + xor(my_x, k)}
        return {"blk": xor(my_y, k) * SIDE + my_x}

    def column(ky, kx):
        return pl.multiple_of((xor(my_y, ky) * SIDE + xor(my_x, kx)) * nb, nb)

    def remote(src, dst, send, recv, axis, k):
        return pltpu.make_async_remote_copy(
            src_ref=src, dst_ref=dst, send_sem=send, recv_sem=recv, device_id=peer(axis, k), device_id_type=MESH
        )

    def own_copy(at):
        ky, kx = LOCAL[at]
        return pltpu.make_async_copy(factor.at[:, pl.ds(column(ky, kx), nb)], own_blocks.at[at], own_sem.at[at])

    initial_copy = pltpu.make_async_copy(initial, staged, own_sem.at[len(LOCAL)])
    initial_copy.start()
    for at in range(len(LOCAL)):
        own_copy(at).start()

    barrier = pltpu.get_barrier_semaphore()
    for axis in (X, Y):
        for k in (1, 2, 3):
            pl.semaphore_signal(barrier, inc=1, device_id=peer(axis, k), device_id_type=MESH)

    low_end, high_end = bounds[0], bounds[1]
    centre = (low_end + high_end) / 2.0
    radius = (high_end - low_end) / 2.0
    scale = 2.0 / radius

    def put(axis, k_out, k_in, rows, columns, value):
        high, low = split(value)
        w_high[axis, k_out, pl.ds(k_in * nb + rows[0], rows[1]), pl.ds(columns[0], columns[1])] = high
        w_low[axis, k_out, pl.ds(k_in * nb + rows[0], rows[1]), pl.ds(columns[0], columns[1])] = low

    whole = (0, nb)

    def place(ky, kx, value, axis):
        value = value * scale
        if axis == X:
            put(Y, ky, kx, whole, whole, value)
            put(X, kx, ky, whole, whole, value.T)
        else:
            put(X, kx, ky, whole, whole, value)
            put(Y, ky, kx, whole, whole, value.T)

    initial_copy.wait()
    start[...] = staged[...].T
    for chain in range(CHAINS):
        vectors[chain, FIRST[chain]] = jnp.zeros((kc, SIDE * nb), F32)

    pl.semaphore_wait(barrier, 6)

    def rows_of(chain):
        return pl.ds(chain * kc, kc)

    def slot(k):
        return pl.ds(k * nb, nb)

    def first_copy(chain, k):
        axis = 1 - FIRST[chain]
        return remote(
            start.at[rows_of(chain)], vectors.at[chain, axis, :, slot(k)],
            last_send.at[0, chain, k], last_recv.at[0, chain, k], axis, k,
        )

    def last_copy(chain, k):
        axis = FIRST[chain]
        return remote(
            partial.at[chain, axis, :, slot(k)], last_in.at[chain, k],
            last_send.at[1, chain, k], last_recv.at[1, chain, k], axis, k,
        )

    def block_copy(ky, kx, axis):
        return remote(
            factor.at[:, pl.ds(column(ky, kx), nb)], arrived.at[ky, kx],
            block_send.at[ky, kx], block_recv.at[ky, kx], axis, kx if axis == X else ky,
        )

    top_copy = remote(
        factor.at[pl.ds(0, half), pl.ds(column(2, 2), nb)], arrived.at[2, 2, pl.ds(0, half)],
        block_send.at[2, 2], block_recv.at[2, 2], X, 2,
    )
    side_copy = remote(
        factor.at[:, pl.ds(pl.multiple_of(column(2, 2) + half, half), half)], arrived_half,
        block_send.at[0, 0], block_recv.at[0, 0], Y, 2,
    )

    for chain in range(CHAINS):
        for k in (2, 1, 3):
            first_copy(chain, k).start()
    block_copies = []
    for over_x, over_y in zip(OVER_X, OVER_Y):
        block_copies += [(over_x, X), (over_y, Y)]
    for (ky, kx), axis in block_copies:
        block_copy(ky, kx, axis).start()
    top_copy.start()
    side_copy.start()

    for at, (ky, kx) in enumerate(LOCAL):
        own_copy(at).wait()
        value = own_blocks[at]
        if at == 0:
            row_at = lax.broadcasted_iota(jnp.int32, (nb, nb), 0)
            column_at = lax.broadcasted_iota(jnp.int32, (nb, nb), 1)
            value = jnp.where(row_at == column_at, value - centre, value)
        place(ky, kx, value, X if kx == 0 else Y)

    def stack(chain, k, value):
        high, low = split(value)
        stacked[chain, pl.ds(0, kc), slot(k)] = high
        stacked[chain, pl.ds(kc, kc), slot(k)] = low

    for chain in range(CHAINS):
        axis = 1 - FIRST[chain]
        vectors[chain, axis, :, slot(0)] = start[rows_of(chain)]
        for k in (1, 3, 2):
            first_copy(chain, k).wait()
        for k in range(SIDE):
            stack(chain, k, vectors[chain, axis, :, slot(k)])
    for (ky, kx), axis in block_copies:
        block_copy(ky, kx, axis).wait_recv()
        place(ky, kx, arrived[ky, kx], axis)
    top_copy.wait_recv()
    top = arrived[2, 2, pl.ds(0, half)] * scale
    put(Y, 2, 2, (0, half), whole, top)
    put(X, 2, 2, whole, (0, half), top.T)
    side_copy.wait_recv()
    side = arrived_half[...] * scale
    put(X, 2, 2, whole, (half, half), side)
    put(Y, 2, 2, (half, half), whole, side.T)

    def parts():
        return ((0, 1, 3), (1, 3, 1))

    def exchange(chain, axis, order, stage, part):
        which, first, second = parts()[part]
        rows = pl.ds(which * hc, hc)
        source = (partial, sums)[stage].at[chain, axis, rows]
        target = (from_first, from_second)[stage].at[order % 4, chain, rows]
        return remote(
            source, target, x_send.at[order % 4, chain, stage, part], x_recv.at[order % 4, chain, stage, part],
            axis, (first, second)[stage],
        )

    def multiply(chain, axis, send):
        for k in (1, 2, 3, 0):
            both = lax.dot_general(stacked[chain], w_high[axis, k], NN, preferred_element_type=F32)
            rest = lax.dot_general(stacked[chain, pl.ds(0, kc)], w_low[axis, k], NN, preferred_element_type=F32)
            partial[chain, axis, :, slot(k)] = both[:kc] + (both[kc:] + rest)
            if send is None and k:
                last_copy(chain, k).start()
        if send is not None:
            for part in (0, 1):
                exchange(chain, axis, send, 0, part).start()

    def middle(chain, axis, order):
        for part, (which, first, _) in enumerate(parts()):
            rows = pl.ds(which * hc, hc)
            exchange(chain, axis, order, 0, part).wait_recv()
            for k in range(SIDE):
                sums[chain, axis, rows, slot(k)] = (
                    partial[chain, axis, rows, slot(k)] + from_first[order % 4, chain, rows, slot(k ^ first)]
                )
            exchange(chain, axis, order, 1, part).start()

    def advance(chain, axis, order, factor_of):
        for part, (which, _, second) in enumerate(parts()):
            rows = pl.ds(which * hc, hc)
            exchange(chain, axis, order, 1, part).wait_recv()
            for k in range(SIDE):
                product = sums[chain, axis, rows, slot(k)] + from_second[order % 4, chain, rows, slot(k ^ second)]
                value = factor_of * product - vectors[chain, axis, rows, slot(k)]
                vectors[chain, axis, rows, slot(k)] = value
                high, low = split(value)
                stacked[chain, rows, slot(k)] = high
                stacked[chain, pl.ds(kc + which * hc, hc), slot(k)] = low

    def settle(chain, axis, order):
        for stage in (0, 1):
            for part in (0, 1):
                exchange(chain, axis, order, stage, part).wait_send()

    def axis_of(chain, later):
        return (FIRST[chain] + later) % 2

    for chain in range(CHAINS):
        multiply(chain, FIRST[chain], 0)

    def pair(step, carry):
        order = 2 * step
        factor_of = jnp.where(step == 0, 0.5, 1.0)
        for chain in range(CHAINS):
            middle(chain, axis_of(chain, 0), order)
        for chain in range(CHAINS):
            advance(chain, axis_of(chain, 0), order, factor_of)
            multiply(chain, axis_of(chain, 1), order + 1)
            settle(chain, axis_of(chain, 0), order)
        for chain in range(CHAINS):
            middle(chain, axis_of(chain, 1), order + 1)

        if isinstance(step, int):
            return carry
        for chain in range(CHAINS):
            advance(chain, axis_of(chain, 1), order + 1, 1.0)
            multiply(chain, axis_of(chain, 0), order + 2)
            settle(chain, axis_of(chain, 1), order + 1)
        return carry

    lax.fori_loop(0, DEGREE // 2 - 1, pair, 0)
    pair(DEGREE // 2 - 1, 0)
    for chain in range(CHAINS):
        advance(chain, axis_of(chain, 1), DEGREE - 1, 1.0)
        start[rows_of(chain)] = vectors[chain, axis_of(chain, 1), :, slot(0)]

    hk = k_all // 2

    def small_copy(which, stage, part, k):
        axis = (part + stage) % 2
        return remote(
            small_out.at[which, stage, pl.ds(part * hk, hk)], small_in.at[which, stage, k, pl.ds(part * hk, hk)],
            small_send.at[which, stage, part, k], small_recv.at[which, stage, part, k], axis, k,
        )

    def small_start(which, stage):
        for k in (2, 1, 3):
            for part in (0, 1):
                small_copy(which, stage, part, k).start()

    def small_sum(which, stage):
        for k in (1, 3, 2):
            for part in (0, 1):
                small_copy(which, stage, part, k).wait_recv()
        return (small_out[which, stage] + small_in[which, stage, 1]) + (small_in[which, stage, 2] + small_in[which, stage, 3])

    filtered = start[...]
    small_out[0, 0] = exact_dot(filtered, filtered, NT)
    small_start(0, 0)
    for chain in range(CHAINS):
        multiply(chain, FIRST[chain], None)
        settle(chain, axis_of(chain, 1), DEGREE - 1)
    small_out[0, 1] = small_sum(0, 0)
    small_start(0, 1)
    for chain in range(CHAINS):
        for k in (1, 3, 2):
            last_copy(chain, k).wait_recv()
        product = (partial[chain, FIRST[chain], :, slot(0)] + last_in[chain, 1]) + (last_in[chain, 2] + last_in[chain, 3])
        image_own[rows_of(chain)] = product
    image = image_own[...] * (0.5 * radius) + centre * filtered
    small_out[1, 0] = exact_dot(filtered * DOWN, image * DOWN, NT)
    small_start(1, 0)
    gram = small_sum(0, 1)

    row_at = lax.broadcasted_iota(jnp.int32, (k_all, k_all), 0)
    column_at = lax.broadcasted_iota(jnp.int32, (k_all, k_all), 1)

    work[:, pl.ds(0, k_all)] = gram
    work[:, pl.ds(k_all, k_all)] = jnp.where(row_at == column_at, 1.0, 0.0)
    panel_row = lax.broadcasted_iota(jnp.int32, (PANEL, k_all), 0)

    def eliminate(panel):
        rows = pl.ds(panel * PANEL, PANEL)
        left, right = work[rows, pl.ds(0, k_all)], work[rows, pl.ds(k_all, k_all)]
        for group in range(0, PANEL, GROUP):
            at = panel * PANEL + group
            spread = [jnp.broadcast_to(left[:, at + t : at + t + 1], (PANEL, k_all)) for t in range(GROUP)]
            for t in range(GROUP):
                j = group + t
                inverse = lax.rsqrt(spread[t][j : j + 1, :])
                multiplier = jnp.where(panel_row > j, spread[t], 0.0) * inverse
                for later in range(t + 1, GROUP):
                    spread[later] = spread[later] - multiplier * (spread[later][j : j + 1, :] * inverse)
                left_row, right_row = left[j : j + 1, :] * inverse, right[j : j + 1, :] * inverse
                left = jnp.where(panel_row == j, left_row, left - multiplier * left_row)
                right = jnp.where(panel_row == j, right_row, right - multiplier * right_row)
        work[rows, pl.ds(0, k_all)] = left
        work[rows, pl.ds(k_all, k_all)] = right
        done = (panel + 1) * PANEL
        if done < k_all:
            below = pl.ds(done, k_all - done)
            work[below, :] = work[below, :] - exact_dot(left[:, done:k_all], work[rows, :], TN)

    panels = k_all // PANEL
    for panel in range(panels // 2):
        eliminate(panel)
    small_out[1, 1] = small_sum(1, 0)
    small_start(1, 1)
    for panel in range(panels // 2, panels):
        eliminate(panel)
    inverse_low = work[:, pl.ds(k_all, k_all)]
    basis = exact_dot(inverse_low, filtered, NN)
    mapped = exact_dot(inverse_low, image, NN)
    basis_out[...] = basis.T
    inner = small_sum(1, 1)
    projected = exact_dot(exact_dot(inverse_low / DOWN, inner, NN), inverse_low / DOWN, NT)
    projected_out[...] = projected
    residual_out[...] = (mapped - exact_dot(projected, basis, TN)).T

    for (ky, kx), axis in block_copies:
        block_copy(ky, kx, axis).wait_send()
    top_copy.wait_send()
    side_copy.wait_send()
    for chain in range(CHAINS):
        for k in (1, 2, 3):
            last_copy(chain, k).wait_send()
    for which in (0, 1):
        for stage in (0, 1):
            for part in (0, 1):
                for k in (1, 2, 3):
                    small_copy(which, stage, part, k).wait_send()


def local(factor, initial, bounds):
    nb, k_all = initial.shape
    kc = k_all // CHAINS
    vmem = pl.BlockSpec(memory_space=pltpu.VMEM)
    hbm = pl.BlockSpec(memory_space=pltpu.HBM)
    dma = pltpu.SemaphoreType.DMA
    long = SIDE * nb
    return pl.pallas_call(
        kernel,
        out_shape=(
            jax.ShapeDtypeStruct((nb, k_all), F32),
            jax.ShapeDtypeStruct((k_all, k_all), F32),
            jax.ShapeDtypeStruct((nb, k_all), F32),
        ),
        in_specs=[hbm, hbm, pl.BlockSpec(memory_space=pltpu.SMEM)],
        out_specs=(vmem, vmem, vmem),
        scratch_shapes=[
            pltpu.VMEM((len(LOCAL), nb, nb), F32),
            pltpu.VMEM((SIDE, SIDE, nb, nb), F32),
            pltpu.VMEM((nb, nb // 2), F32),
            pltpu.VMEM((k_all, nb), F32),
            pltpu.VMEM((2, SIDE, long, nb), BF16),
            pltpu.VMEM((2, SIDE, long, nb), BF16),
            pltpu.VMEM((CHAINS, 2, kc, long), F32),
            pltpu.VMEM((CHAINS, 2 * kc, long), BF16),
            pltpu.VMEM((CHAINS, 2, kc, long), F32),
            pltpu.VMEM((CHAINS, 2, kc, long), F32),
            pltpu.VMEM((4, CHAINS, kc, long), F32),
            pltpu.VMEM((4, CHAINS, kc, long), F32),
            pltpu.VMEM((CHAINS, SIDE, kc, nb), F32),
            pltpu.VMEM((k_all, nb), F32),
            pltpu.VMEM((2, 2, k_all, k_all), F32),
            pltpu.VMEM((2, 2, SIDE, k_all, k_all), F32),
            pltpu.VMEM((k_all, 2 * k_all), F32),
            pltpu.VMEM((nb, k_all), F32),
            dma((len(LOCAL) + 1,)),
            dma((SIDE, SIDE)),
            dma((SIDE, SIDE)),
            dma((4, CHAINS, 2, 2)),
            dma((4, CHAINS, 2, 2)),
            dma((2, CHAINS, SIDE)),
            dma((2, CHAINS, SIDE)),
            dma((2, 2, 2, SIDE)),
            dma((2, 2, 2, SIDE)),
        ],
        compiler_params=pltpu.CompilerParams(collective_id=0, has_side_effects=True, vmem_limit_bytes=61 << 20),
    )(factor, initial, bounds)


def solution(mesh):
    in_specs = (P(("bulk", "blk"), None), P(("bulk", "blk"), None), P("bulk"))
    out_specs = (P(("bulk", "blk"), None), P("bulk", None), P(("bulk", "blk"), None))
    return jax.shard_map(local, mesh=mesh, in_specs=in_specs, out_specs=out_specs, check_vma=False)
```

time: 149 us -> 127 us (0.85)
  Pallas kernels: 142 us -> 122 us
    pallas_call x1, Pallas kernels: 142 us -> 122 us  [local(): pl.pallas_call(kernel, out_shape=(jax.ShapeDtypeStruct((nb, k_all), F32),...]
    unnamed x9 -> x3, local copies, waits for them, and re-layouts: 5.68 us -> 4.61 us
where the time goes in v2:
time: 127 us
  Pallas kernels  122 us (96%)
  local copies, waits for them, and re-layouts  4.61 us (4%)
    pallas_call x1, Pallas kernels, local(): pl.pallas_call(kernel, out_shape=(jax.ShapeDtypeStruct((nb, k_all), F32),...  122 us
    unnamed x3, local copies, waits for them, and re-layouts  4.61 us

profile of v2, /device:TPU:448, one launch (start us, length us, event | category | flops | bytes accessed | tf_op | source)
XLA Modules:
  0.0 127.2 jit_solution(7607706539583389702)
XLA Ops:
  0.6 121.9 %shard_map.58 = (f32[256,128]{1,0:T(8,128)}, f32[128,128]{1,0:T(8,128)}, f32[256,128]{1,0:T(8,128)}) custom-call(f32[256,4096]{1,0:T(8,128)} %factor.1, f32[256,128]{1,0:T(8,128)} %initial.1, f32[2]{0:T(128)} %bounds.1), custom_call_target="tpu_custom_call" | custom-call | tf_op jit(solution)/shard_map/pallas_call | solution.py:385
  122.6 1.6 %copy.9 = f32[256,128]{1,0:T(8,128)} copy(f32[256,128]{1,0:T(8,128)} %get-tuple-element.6) | data formatting | bytes 262144
  124.1 1.5 %copy.10 = f32[128,128]{1,0:T(8,128)} copy(f32[128,128]{1,0:T(8,128)} %get-tuple-element.7) | data formatting | bytes 131072
  125.6 1.6 %copy.11 = f32[256,128]{1,0:T(8,128)} copy(f32[256,128]{1,0:T(8,128)} %get-tuple-element.8) | data formatting | bytes 262144

commit v3 on v2

--- a/solution.py
+++ b/solution.py
@@ -183,18 +183,6 @@
             first_copy(chain, k).wait()
         for k in range(SIDE):
             stack(chain, k, vectors[chain, axis, :, slot(k)])
-    for (ky, kx), axis in block_copies:
-        block_copy(ky, kx, axis).wait_recv()
-        place(ky, kx, arrived[ky, kx], axis)
-    top_copy.wait_recv()
-    top = arrived[2, 2, pl.ds(0, half)] * scale
-    put(Y, 2, 2, (0, half), whole, top)
-    put(X, 2, 2, whole, (0, half), top.T)
-    side_copy.wait_recv()
-    side = arrived_half[...] * scale
-    put(X, 2, 2, whole, (half, half), side)
-    put(Y, 2, 2, (half, half), whole, side.T)
-
     def parts():
         return ((0, 1, 3), (1, 3, 1))
 
@@ -208,14 +196,20 @@
             axis, (first, second)[stage],
         )
 
-    def multiply(chain, axis, send):
-        for k in (1, 2, 3, 0):
+    def dots(chain, axis, slots):
+        for k in slots:
             both = lax.dot_general(stacked[chain], w_high[axis, k], NN, preferred_element_type=F32)
             rest = lax.dot_general(stacked[chain, pl.ds(0, kc)], w_low[axis, k], NN, preferred_element_type=F32)
             partial[chain, axis, :, slot(k)] = both[:kc] + (both[kc:] + rest)
-            if send is None and k:
-                last_copy(chain, k).start()
-        if send is not None:
+
+    def multiply(chain, axis, send):
+        if send is None:
+            for k in (2, 1, 3, 0):
+                dots(chain, axis, (k,))
+                if k:
+                    last_copy(chain, k).start()
+        else:
+            dots(chain, axis, (0, 1, 2, 3))
             for part in (0, 1):
                 exchange(chain, axis, send, 0, part).start()
 
@@ -249,8 +243,24 @@
     def axis_of(chain, later):
         return (FIRST[chain] + later) % 2
 
-    for chain in range(CHAINS):
-        multiply(chain, FIRST[chain], 0)
+    for (ky, kx), axis in block_copies:
+        block_copy(ky, kx, axis).wait_recv()
+        place(ky, kx, arrived[ky, kx], axis)
+    for chain in range(CHAINS):
+        dots(chain, FIRST[chain], (0, 1, 3))
+    top_copy.wait_recv()
+    top = arrived[2, 2, pl.ds(0, half)] * scale
+    put(Y, 2, 2, (0, half), whole, top)
+    put(X, 2, 2, whole, (0, half), top.T)
+    side_copy.wait_recv()
+    side = arrived_half[...] * scale
+    put(X, 2, 2, whole, (half, half), side)
+    put(Y, 2, 2, (half, half), whole, side.T)
+
+    for chain in range(CHAINS):
+        dots(chain, FIRST[chain], (2,))
+        for part in (0, 1):
+            exchange(chain, FIRST[chain], 0, 0, part).start()
 
     def pair(step, carry):
         order = 2 * step
@@ -420,7 +430,7 @@
             dma((2, 2, 2, SIDE)),
             dma((2, 2, 2, SIDE)),
         ],
-        compiler_params=pltpu.CompilerParams(collective_id=0, has_side_effects=True, vmem_limit_bytes=61 << 20),
+        compiler_params=pltpu.CompilerParams(collective_id=0, has_side_effects=True, vmem_limit_bytes=52 << 20),
     )(factor, initial, bounds)
 
 

time: 127 us -> 125 us (0.984)
  the two profiles are of different devices: /device:TPU:448 before, /device:TPU:320 now
where the time goes in v3:
time: 125 us
  Pallas kernels  121 us (97%)
  local copies, waits for them, and re-layouts  3.49 us (3%)
    pallas_call x1, Pallas kernels, local(): pl.pallas_call(kernel, out_shape=(jax.ShapeDtypeStruct((nb, k_all), F32),...  121 us
    unnamed x7, local copies, waits for them, and re-layouts  3.49 us

profile of v3, /device:TPU:320, one launch (start us, length us, event | category | flops | bytes accessed | tf_op | source)
XLA Modules:
  0.0 124.8 jit_solution(9574972241522501663)
XLA Ops:
  0.6 0.0 copy-start
  0.6 0.9 copy-done
  1.5 0.0 copy-start.1
  1.5 0.7 copy-done.1
  2.2 120.6 %shard_map.58 = (f32[256,128]{1,0:T(8,128)S(1)}, f32[128,128]{1,0:T(8,128)S(1)}, f32[256,128]{1,0:T(8,128)S(1)}) custom-call(f32[256,4096]{1,0:T(8,128)} %factor.1, f32[256,128]{1,0:T(8,128)S(1)} %copy-done, f32[2]{0:T(128)S(1)} %copy-done.1), custom_call_target="tpu_custom_call" | custom-call | tf_op jit(solution)/shard_map/pallas_call | solution.py:395
  122.8 0.7 copy.9
  123.5 0.6 copy.10
  124.1 0.7 copy.11
Async XLA Ops:
  0.6 0.9 copy-start
  1.5 0.7 copy-start.1

commit v4 on v3

--- a/solution.py
+++ b/solution.py
@@ -189,11 +189,12 @@
     def exchange(chain, axis, order, stage, part):
         which, first, second = parts()[part]
         rows = pl.ds(which * hc, hc)
-        source = (partial, sums)[stage].at[chain, axis, rows]
-        target = (from_first, from_second)[stage].at[order % 4, chain, rows]
+        lanes = pl.ds((stage // 2) * 2 * nb, 2 * nb)
+        source = (partial, sums)[stage % 2].at[chain, axis, rows, lanes]
+        target = (from_first, from_second)[stage % 2].at[order % 4, chain, rows, lanes]
         return remote(
             source, target, x_send.at[order % 4, chain, stage, part], x_recv.at[order % 4, chain, stage, part],
-            axis, (first, second)[stage],
+            axis, (first, second)[stage % 2],
         )
 
     def dots(chain, axis, slots):
@@ -209,24 +210,28 @@
                 if k:
                     last_copy(chain, k).start()
         else:
-            dots(chain, axis, (0, 1, 2, 3))
-            for part in (0, 1):
-                exchange(chain, axis, send, 0, part).start()
+            for piece in (0, 2):
+                dots(chain, axis, (piece, piece + 1))
+                for part in (0, 1):
+                    exchange(chain, axis, send, piece, part).start()
 
     def middle(chain, axis, order):
-        for part, (which, first, _) in enumerate(parts()):
-            rows = pl.ds(which * hc, hc)
-            exchange(chain, axis, order, 0, part).wait_recv()
-            for k in range(SIDE):
-                sums[chain, axis, rows, slot(k)] = (
-                    partial[chain, axis, rows, slot(k)] + from_first[order % 4, chain, rows, slot(k ^ first)]
-                )
-            exchange(chain, axis, order, 1, part).start()
+        for piece in (0, 1):
+            for part, (which, first, _) in enumerate(parts()):
+                rows = pl.ds(which * hc, hc)
+                exchange(chain, axis, order, 2 * piece, part).wait_recv()
+                mine = piece if first == 1 else 1 - piece
+                for k in (2 * mine, 2 * mine + 1):
+                    sums[chain, axis, rows, slot(k)] = (
+                        partial[chain, axis, rows, slot(k)] + from_first[order % 4, chain, rows, slot(k ^ first)]
+                    )
+                exchange(chain, axis, order, 2 * mine + 1, part).start()
 
     def advance(chain, axis, order, factor_of):
         for part, (which, _, second) in enumerate(parts()):
             rows = pl.ds(which * hc, hc)
             exchange(chain, axis, order, 1, part).wait_recv()
+            exchange(chain, axis, order, 3, part).wait_recv()
             for k in range(SIDE):
                 product = sums[chain, axis, rows, slot(k)] + from_second[order % 4, chain, rows, slot(k ^ second)]
                 value = factor_of * product - vectors[chain, axis, rows, slot(k)]
@@ -236,7 +241,7 @@
                 stacked[chain, pl.ds(kc + which * hc, hc), slot(k)] = low
 
     def settle(chain, axis, order):
-        for stage in (0, 1):
+        for stage in range(4):
             for part in (0, 1):
                 exchange(chain, axis, order, stage, part).wait_send()
 
@@ -261,6 +266,7 @@
         dots(chain, FIRST[chain], (2,))
         for part in (0, 1):
             exchange(chain, FIRST[chain], 0, 0, part).start()
+            exchange(chain, FIRST[chain], 0, 2, part).start()
 
     def pair(step, carry):
         order = 2 * step
@@ -270,6 +276,7 @@
         for chain in range(CHAINS):
             advance(chain, axis_of(chain, 0), order, factor_of)
             multiply(chain, axis_of(chain, 1), order + 1)
+        for chain in range(CHAINS):
             settle(chain, axis_of(chain, 0), order)
         for chain in range(CHAINS):
             middle(chain, axis_of(chain, 1), order + 1)
@@ -279,6 +286,7 @@
         for chain in range(CHAINS):
             advance(chain, axis_of(chain, 1), order + 1, 1.0)
             multiply(chain, axis_of(chain, 0), order + 2)
+        for chain in range(CHAINS):
             settle(chain, axis_of(chain, 1), order + 1)
         return carry
 
@@ -313,6 +321,7 @@
     small_start(0, 0)
     for chain in range(CHAINS):
         multiply(chain, FIRST[chain], None)
+    for chain in range(CHAINS):
         settle(chain, axis_of(chain, 1), DEGREE - 1)
     small_out[0, 1] = small_sum(0, 0)
     small_start(0, 1)
@@ -423,8 +432,8 @@
             dma((len(LOCAL) + 1,)),
             dma((SIDE, SIDE)),
             dma((SIDE, SIDE)),
-            dma((4, CHAINS, 2, 2)),
-            dma((4, CHAINS, 2, 2)),
+            dma((4, CHAINS, 4, 2)),
+            dma((4, CHAINS, 4, 2)),
             dma((2, CHAINS, SIDE)),
             dma((2, CHAINS, SIDE)),
             dma((2, 2, 2, SIDE)),

time: 125 us -> 123 us (0.984)
  the two profiles are of different devices: /device:TPU:320 before, /device:TPU:160 now
where the time goes in v4:
time: 123 us
  Pallas kernels  119 us (97%)
  local copies, waits for them, and re-layouts  3.49 us (3%)
    pallas_call x1, Pallas kernels, local(): pl.pallas_call(kernel, out_shape=(jax.ShapeDtypeStruct((nb, k_all), F32),...  119 us
    unnamed x7, local copies, waits for them, and re-layouts  3.49 us

profile of v4, /device:TPU:160, one launch (start us, length us, event | category | flops | bytes accessed | tf_op | source)
XLA Modules:
  0.0 122.7 jit_solution(9090280028681187865)
XLA Ops:
  0.6 0.0 copy-start
  0.6 0.9 copy-done
  1.5 0.0 copy-start.1
  1.5 0.7 copy-done.1
  2.2 118.5 %shard_map.58 = (f32[256,128]{1,0:T(8,128)S(1)}, f32[128,128]{1,0:T(8,128)S(1)}, f32[256,128]{1,0:T(8,128)S(1)}) custom-call(f32[256,4096]{1,0:T(8,128)} %factor.1, f32[256,128]{1,0:T(8,128)S(1)} %copy-done, f32[2]{0:T(128)S(1)} %copy-done.1), custom_call_target="tpu_custom_call" | custom-call | tf_op jit(solution)/shard_map/pallas_call | solution.py:404
  120.7 0.7 copy.9
  121.4 0.6 copy.10
  122.0 0.7 copy.11
Async XLA Ops:
  0.6 0.9 copy-start
  1.5 0.7 copy-start.1

commit v5 on v4

--- a/solution.py
+++ b/solution.py
@@ -78,15 +78,15 @@
         ky, kx = LOCAL[at]
         return pltpu.make_async_copy(factor.at[:, pl.ds(column(ky, kx), nb)], own_blocks.at[at], own_sem.at[at])
 
+    barrier = pltpu.get_barrier_semaphore()
+    for axis in (X, Y):
+        for k in (1, 2, 3):
+            pl.semaphore_signal(barrier, inc=1, device_id=peer(axis, k), device_id_type=MESH)
+
     initial_copy = pltpu.make_async_copy(initial, staged, own_sem.at[len(LOCAL)])
     initial_copy.start()
     for at in range(len(LOCAL)):
         own_copy(at).start()
-
-    barrier = pltpu.get_barrier_semaphore()
-    for axis in (X, Y):
-        for k in (1, 2, 3):
-            pl.semaphore_signal(barrier, inc=1, device_id=peer(axis, k), device_id_type=MESH)
 
     low_end, high_end = bounds[0], bounds[1]
     centre = (low_end + high_end) / 2.0
@@ -228,17 +228,18 @@
                 exchange(chain, axis, order, 2 * mine + 1, part).start()
 
     def advance(chain, axis, order, factor_of):
-        for part, (which, _, second) in enumerate(parts()):
-            rows = pl.ds(which * hc, hc)
-            exchange(chain, axis, order, 1, part).wait_recv()
-            exchange(chain, axis, order, 3, part).wait_recv()
-            for k in range(SIDE):
-                product = sums[chain, axis, rows, slot(k)] + from_second[order % 4, chain, rows, slot(k ^ second)]
-                value = factor_of * product - vectors[chain, axis, rows, slot(k)]
-                vectors[chain, axis, rows, slot(k)] = value
-                high, low = split(value)
-                stacked[chain, rows, slot(k)] = high
-                stacked[chain, pl.ds(kc + which * hc, hc), slot(k)] = low
+        for piece in (0, 1):
+            for part, (which, _, second) in enumerate(parts()):
+                rows = pl.ds(which * hc, hc)
+                mine = piece if second == 1 else 1 - piece
+                exchange(chain, axis, order, 2 * piece + 1, part).wait_recv()
+                for k in (2 * mine, 2 * mine + 1):
+                    product = sums[chain, axis, rows, slot(k)] + from_second[order % 4, chain, rows, slot(k ^ second)]
+                    value = factor_of * product - vectors[chain, axis, rows, slot(k)]
+                    vectors[chain, axis, rows, slot(k)] = value
+                    high, low = split(value)
+                    stacked[chain, rows, slot(k)] = high
+                    stacked[chain, pl.ds(kc + which * hc, hc), slot(k)] = low
 
     def settle(chain, axis, order):
         for stage in range(4):

time: 123 us -> 123 us (level)
  the two profiles are of different devices: /device:TPU:160 before, /device:TPU:448 now
where the time goes in v5:
time: 123 us
  Pallas kernels  119 us (97%)
  local copies, waits for them, and re-layouts  3.49 us (3%)
    pallas_call x1, Pallas kernels, local(): pl.pallas_call(kernel, out_shape=(jax.ShapeDtypeStruct((nb, k_all), F32),...  119 us
    unnamed x7, local copies, waits for them, and re-layouts  3.49 us

profile of v5, /device:TPU:448, one launch (start us, length us, event | category | flops | bytes accessed | tf_op | source)
XLA Modules:
  0.0 122.7 jit_solution(10508665561582582435)
XLA Ops:
  0.6 0.0 copy-start
  0.6 0.9 copy-done
  1.5 0.0 copy-start.1
  1.5 0.7 copy-done.1
  2.2 118.5 %shard_map.58 = (f32[256,128]{1,0:T(8,128)S(1)}, f32[128,128]{1,0:T(8,128)S(1)}, f32[256,128]{1,0:T(8,128)S(1)}) custom-call(f32[256,4096]{1,0:T(8,128)} %factor.1, f32[256,128]{1,0:T(8,128)S(1)} %copy-done, f32[2]{0:T(128)S(1)} %copy-done.1), custom_call_target="tpu_custom_call" | custom-call | tf_op jit(solution)/shard_map/pallas_call | solution.py:405
  120.7 0.7 copy.9
  121.4 0.6 copy.10
  122.0 0.7 copy.11
Async XLA Ops:
  0.6 0.9 copy-start
  1.5 0.7 copy-start.1
